TPU v7x, 32 devices: a whole 2x2x4 slice. The times are simulated.
32 devices in a mesh: shard: 8 (over z, x), rep: 4 (over y, core).
Axes of the slice: x: 2, y: 2, z: 4, core: 2. Of those that a mesh axis runs over, the one named last changes fastest.
Arguments:
- images: bfloat16 [32, 197, 768], P(('shard', 'rep')), may hold values from -6 to 6
- cotangent: bfloat16 [32, 197, 768], P(('shard', 'rep')), may hold values from -6 to 6
- weights_in: float32 [768, 6144], P('shard'), may hold values from -13 to 13
- weights_down: float32 [3072, 768], P('shard'), may hold values from -0.109375 to 0.109375
- vectors: float32 [12, 768], P(None, 'shard'), may hold values from -1.5 to 1.5, as said below
- mean_in: float32 [768, 6144], P('shard'), may hold values from -256 to 256
- mean_down: float32 [3072, 768], P('shard'), may hold values from -256 to 256
- mean_vectors: float32 [12, 768], P(None, 'shard'), may hold values from -256 to 256
- square_in: float32 [768, 6144], P('shard'), may hold values from 63.04 to 6304
- square_down: float32 [3072, 768], P('shard'), may hold values from 63.04 to 6304
- square_vectors: float32 [12, 768], P(None, 'shard'), may hold values from 63.04 to 6304
Outputs:
- block_out: bfloat16 [32, 197, 768], P(('shard', 'rep'))
- input_grad: float32 [32, 197, 768], P(('shard', 'rep'))
- grad_in: float32 [768, 6144], P('shard')
- grad_down: float32 [3072, 768], P('shard')
- grad_vectors: float32 [12, 768], P(None, 'shard')
- updated_in: float32 [768, 6144], P('shard')
- updated_down: float32 [3072, 768], P('shard')
- updated_vectors: float32 [12, 768], P(None, 'shard')
- next_mean_in: float32 [768, 6144], P('shard')
- next_mean_down: float32 [3072, 768], P('shard')
- next_mean_vectors: float32 [12, 768], P(None, 'shard')
- next_square_in: float32 [768, 6144], P('shard')
- next_square_down: float32 [3072, 768], P('shard')
- next_square_vectors: float32 [12, 768], P(None, 'shard')
Inputs may be any that keep to these rules, and one draw needn't show every extreme that they name: `vectors`: rows 0 and 5 are the norms' gains.
All inputs are finite; a program needn't handle non-finite values.
Results may differ from a plain program's by a relative error of at most 0.023.
Values may be sent and summed in bfloat16 or wider, within the bound.
A program may use at most 128 MiB of HBM per device.

v0:
```python
import math
import jax
import jax.numpy as jnp
from jax import lax
from jax.sharding import PartitionSpec as P

HEADS = 12
NORM_EPS = 1e-06
BETA_ONE = 0.9
BETA_TWO = 0.95
ADAM_EPS = 1e-08
RATE_MATRIX = 0.008
RATE_VECTOR = 0.15
DECAY_MATRIX = 0.05
STEP_COUNT = 2.0


def to_half(array_in):
    return array_in.astype(jnp.bfloat16)


def matmul(left, right):
    return jnp.dot(left, right, preferred_element_type=jnp.float32)


def times_transposed(left, right):
    return lax.dot_general(
        left, right, (((1,), (1,)), ((), ())), preferred_element_type=jnp.float32
    )


def transposed_times(left, right):
    return lax.dot_general(
        left, right, (((0,), (0,)), ((), ())), preferred_element_type=jnp.float32
    )


def layer_norm(inputs, gain, shift):
    centred = inputs - jnp.mean(inputs, axis=-1, keepdims=True)
    inv_std = lax.rsqrt(jnp.mean(centred * centred, axis=-1, keepdims=True) + NORM_EPS)
    normed = centred * inv_std
    return (normed, inv_std, normed * gain + shift)


def norm_back(grad_after, normed, inv_std, gain):
    grad_normed = grad_after * gain
    grad_inputs = inv_std * (
        grad_normed
        - jnp.mean(grad_normed, axis=-1, keepdims=True)
        - normed * jnp.mean(grad_normed * normed, axis=-1, keepdims=True)
    )
    return (grad_inputs, jnp.sum(grad_after * normed, axis=0), jnp.sum(grad_after, axis=0))


def gaussian_unit(hidden):
    cdf_part = 0.5 * (1.0 + jax.scipy.special.erf(hidden * 0.7071067811865476))
    slope = cdf_part + hidden * jnp.exp(-0.5 * hidden * hidden) * 0.3989422804014327
    return (hidden * cdf_part, slope)


def head_scores(query_heads, key_heads, score_scale):
    return (
        jnp.einsum("bqhe,bkhe->bhqk", query_heads, key_heads, preferred_element_type=jnp.float32)
        * score_scale
    )


def forward_pass(images, matrix_half, down_half, vector_half):
    img_count, seq_len, model_width = images.shape
    head_dim = model_width // HEADS
    score_scale = 1.0 / math.sqrt(head_dim)
    row_count = img_count * seq_len
    head_shape = (img_count, seq_len, HEADS, head_dim)
    vector_float = vector_half.astype(jnp.float32)
    flat_in = images.reshape(row_count, model_width).astype(jnp.float32)
    normed_one, inv_one, pre_one = layer_norm(flat_in, vector_float[0], vector_float[1])
    act_one = to_half(pre_one)
    projected = matmul(act_one, matrix_half[:, : 3 * model_width])
    query_heads = to_half(projected[:, :model_width] + vector_float[2]).reshape(head_shape)
    key_heads = to_half(projected[:, model_width : 2 * model_width]).reshape(head_shape)
    value_heads = to_half(projected[:, 2 * model_width :] + vector_float[3]).reshape(head_shape)
    scores = head_scores(query_heads, key_heads, score_scale)
    log_total = jax.nn.logsumexp(scores, axis=-1, keepdims=True)
    probs_half = to_half(jnp.exp(scores - log_total))
    attended = to_half(
        jnp.einsum(
            "bhqk,bkhe->bqhe", probs_half, value_heads, preferred_element_type=jnp.float32
        ).reshape(row_count, model_width)
    )
    hidden_one = (
        flat_in
        + matmul(attended, matrix_half[:, 3 * model_width : 4 * model_width])
        + vector_float[4]
    )
    normed_two, inv_two, pre_two = layer_norm(hidden_one, vector_float[5], vector_float[6])
    act_two = to_half(pre_two)
    up_input = matmul(act_two, matrix_half[:, 4 * model_width :]) + vector_float[8:].reshape(-1)
    gelu_out, gelu_slope = gaussian_unit(up_input)
    gelu_half = to_half(gelu_out)
    block_out = to_half(hidden_one + matmul(gelu_half, down_half) + vector_float[7])
    saved = (
        normed_one,
        inv_one,
        act_one,
        query_heads,
        key_heads,
        value_heads,
        log_total,
        attended,
        normed_two,
        inv_two,
        act_two,
        gelu_slope,
        gelu_half,
    )
    return (block_out.reshape(images.shape), saved)


def backward_pass(cotangent, saved, matrix_half, down_half, vector_half):
    (
        normed_one,
        inv_one,
        act_one,
        query_heads,
        key_heads,
        value_heads,
        log_total,
        attended,
        normed_two,
        inv_two,
        act_two,
        gelu_slope,
        gelu_half,
    ) = saved
    img_count, seq_len, model_width = cotangent.shape
    head_dim = model_width // HEADS
    score_scale = 1.0 / math.sqrt(head_dim)
    row_count = img_count * seq_len
    head_shape = (img_count, seq_len, HEADS, head_dim)
    vector_float = vector_half.astype(jnp.float32)
    joint_weights = matrix_half[:, : 3 * model_width]
    output_weights = matrix_half[:, 3 * model_width : 4 * model_width]
    upward_weights = matrix_half[:, 4 * model_width :]
    grad_half = cotangent.reshape(row_count, model_width)
    grad_out = grad_half.astype(jnp.float32)
    grad_up = times_transposed(grad_half, down_half) * gelu_slope
    up_half = to_half(grad_up)
    grad_act_two = times_transposed(up_half, upward_weights)
    grad_norm_two, grad_gain_two, grad_shift_two = norm_back(
        grad_act_two, normed_two, inv_two, vector_float[5]
    )
    grad_hidden = grad_out + grad_norm_two
    hidden_half = to_half(grad_hidden)
    grad_att = to_half(times_transposed(hidden_half, output_weights)).reshape(head_shape)
    prob_float = jnp.exp(head_scores(query_heads, key_heads, score_scale) - log_total)
    probs_half = to_half(prob_float)
    grad_probs = jnp.einsum(
        "bqhe,bkhe->bhqk", grad_att, value_heads, preferred_element_type=jnp.float32
    )
    row_inner = jnp.sum(prob_float * grad_probs, axis=-1, keepdims=True)
    grad_scores = to_half(prob_float * (grad_probs - row_inner) * score_scale)
    grad_query = jnp.einsum(
        "bhqk,bkhe->bqhe", grad_scores, key_heads, preferred_element_type=jnp.float32
    ).reshape(row_count, model_width)
    grad_key = jnp.einsum(
        "bhqk,bqhe->bkhe", grad_scores, query_heads, preferred_element_type=jnp.float32
    ).reshape(row_count, model_width)
    grad_value = jnp.einsum(
        "bhqk,bqhe->bkhe", probs_half, grad_att, preferred_element_type=jnp.float32
    ).reshape(row_count, model_width)
    grad_proj = to_half(jnp.concatenate([grad_query, grad_key, grad_value], axis=1))
    grad_act_one = times_transposed(grad_proj, joint_weights)
    grad_norm_one, grad_gain_one, grad_shift_one = norm_back(
        grad_act_one, normed_one, inv_one, vector_float[0]
    )
    input_grad = (grad_hidden + grad_norm_one).reshape(cotangent.shape)
    grad_down = transposed_times(gelu_half, grad_half)
    small_rows = jnp.stack(
        [
            grad_gain_one,
            grad_shift_one,
            jnp.sum(grad_query, axis=0),
            jnp.sum(grad_value, axis=0),
            jnp.sum(grad_hidden, axis=0),
            grad_gain_two,
            grad_shift_two,
            jnp.sum(grad_out, axis=0),
        ]
    )
    grad_vectors = jnp.concatenate(
        [small_rows, jnp.sum(grad_up, axis=0).reshape(4, model_width)], axis=0
    )
    factors = (act_one, grad_proj, attended, hidden_half, act_two, up_half)
    return (input_grad, grad_down, grad_vectors, factors)


def adam_update(weights, first, second, gradient, rate, decay):
    next_first = BETA_ONE * first + (1.0 - BETA_ONE) * gradient
    next_second = BETA_TWO * second + (1.0 - BETA_TWO) * gradient * gradient
    corr_first = next_first / (1.0 - BETA_ONE**STEP_COUNT)
    corr_second = next_second / (1.0 - BETA_TWO**STEP_COUNT)
    updated = weights - rate * (corr_first / (jnp.sqrt(corr_second) + ADAM_EPS) + decay * weights)
    return (updated, next_first, next_second)


def local(
    images,
    cotangent,
    weights_in,
    weights_down,
    vectors,
    mean_in,
    mean_down,
    mean_vectors,
    square_in,
    square_down,
    square_vectors,
):
    halves = (to_half(weights_in), to_half(weights_down), to_half(vectors))
    forward_set = (
        lax.all_gather(halves[0], "shard", axis=0, tiled=True),
        lax.all_gather(halves[1], "shard", axis=0, tiled=True),
        lax.all_gather(halves[2], "shard", axis=1, tiled=True),
    )
    block_out, saved = forward_pass(images, forward_set[0], forward_set[1], forward_set[2])
    backward_set = (
        lax.all_gather(halves[0], "shard", axis=0, tiled=True),
        lax.all_gather(halves[1], "shard", axis=0, tiled=True),
        lax.all_gather(halves[2], "shard", axis=1, tiled=True),
    )
    input_grad, grad_down_local, grad_vectors_local, factors = backward_pass(
        cotangent, saved, backward_set[0], backward_set[1], backward_set[2]
    )
    act_one, grad_proj, attended, hidden_half, act_two, up_half = factors

    def column_part(activation, gradient):
        return transposed_times(activation, gradient)

    owned_in = lax.psum_scatter(
        jnp.concatenate(
            [
                column_part(act_one, grad_proj),
                column_part(attended, hidden_half),
                column_part(act_two, up_half),
            ],
            axis=1,
        ).astype(jnp.bfloat16),
        "shard",
        scatter_dimension=0,
        tiled=True,
    )
    owned_down, owned_vectors = (
        lax.psum_scatter(
            grad_down_local.astype(jnp.bfloat16), "shard", scatter_dimension=0, tiled=True
        ).astype(jnp.float32),
        lax.psum_scatter(
            grad_vectors_local.astype(jnp.bfloat16), "shard", scatter_dimension=1, tiled=True
        ).astype(jnp.float32),
    )
    grad_in, grad_down, grad_vectors = (
        lax.psum(owned_in, "rep").astype(jnp.float32),
        lax.psum(owned_down.astype(jnp.bfloat16), "rep").astype(jnp.float32),
        lax.psum(owned_vectors.astype(jnp.bfloat16), "rep").astype(jnp.float32),
    )
    new_in = adam_update(weights_in, mean_in, square_in, grad_in, RATE_MATRIX, DECAY_MATRIX)
    new_down = adam_update(
        weights_down, mean_down, square_down, grad_down, RATE_MATRIX, DECAY_MATRIX
    )
    new_vectors = adam_update(vectors, mean_vectors, square_vectors, grad_vectors, RATE_VECTOR, 0.0)
    return (
        block_out,
        input_grad,
        grad_in,
        grad_down,
        grad_vectors,
        new_in[0],
        new_down[0],
        new_vectors[0],
        new_in[1],
        new_down[1],
        new_vectors[1],
        new_in[2],
        new_down[2],
        new_vectors[2],
    )


def solution(mesh):
    placed = (
        P(("shard", "rep"), None, None),
        P(("shard", "rep"), None, None),
        P("shard", None),
        P("shard", None),
        P(None, "shard"),
        P("shard", None),
        P("shard", None),
        P(None, "shard"),
        P("shard", None),
        P("shard", None),
        P(None, "shard"),
    )
    return jax.shard_map(
        local,
        mesh=mesh,
        in_specs=placed,
        out_specs=(
            P(("shard", "rep"), None, None),
            P(("shard", "rep"), None, None),
            P("shard", None),
            P("shard", None),
            P(None, "shard"),
            P("shard", None),
            P("shard", None),
            P(None, "shard"),
            P("shard", None),
            P("shard", None),
            P(None, "shard"),
            P("shard", None),
            P("shard", None),
            P(None, "shard"),
        ),
        check_vma=False,
    )
```

profile of v0, /device:TPU:0, one launch (start us, length us, event | category | flops | bytes accessed | tf_op | source)
XLA Modules:
  0.0 623.4 jit_solution(6696602671923517766)
XLA Ops:
  7.2 2.9 convert_element_type.95
  11.2 33.3 %all-gather = bf16[8,96,12]{1,2,0:T(8,128)(2,1)S(1)} all-gather(bf16[1,96,12]{1,2,0:T(8,128)(2,1)S(1)} %convert_bitcast_fusion.1), channel_id=1, replica_groups=mesh['shard'=8,'rep'=4] {'shard'}, dimensions={0}, use_global_device_ids=true | all-gather | bytes 20736 | tf_op jit(solution)/shard_map/all_gather | solution.py:223
  45.1 105.8 %all-gather.4.cloned.1.call-done = bf16[768,6144]{1,0:T(8,128)(2,1)} async-done(((bf16[96,6144]{1,0:T(8,128)(2,1)}), bf16[768,6144]{1,0:T(8,128)(2,1)}) %all-gather.4.cloned.1.call-update) | async-done | bytes 9437200 | tf_op jit(solution)/shard_map/all_gather | solution.py:221
  150.9 3.0 fusion.10
  160.3 5.4 multiply_convert_fusion.1
  166.7 3.7 convolution_convert_fusion
  170.7 60.5 %all-gather.6.cloned.1.call-done = bf16[3072,768]{1,0:T(8,128)(2,1)} async-done(((bf16[384,768]{1,0:T(8,128)(2,1)}), bf16[3072,768]{1,0:T(8,128)(2,1)}) %all-gather.6.cloned.1.call-update) | async-done | bytes 4718608 | tf_op jit(solution)/shard_map/all_gather | solution.py:222
  231.2 5.0 fusion.90
  236.2 4.7 multiply_reduce_fusion.2
  242.3 2.5 convolution_convert_fusion.5
  246.7 2.5 convolution_convert_fusion.3
  251.6 3.0 fusion.91
  254.6 4.7 fusion.30
  259.3 4.9 fusion.86
  268.7 4.2 pad_maximum_fusion
  274.3 3.6 fusion.56
  278.9 50.0 %reduce-scatter.8.cloned.1.call-done = bf16[384,768]{1,0:T(8,128)(2,1)} async-done(((bf16[3072,768]{1,0:T(8,128)(2,1)}), bf16[384,768]{1,0:T(8,128)(2,1)}) %reduce-scatter.8.cloned.1.call-update) | async-done | bytes 589840 | tf_op jit(solution)/shard_map/reduce_scatter | solution.py:253
  328.9 165.2 %reduce-scatter.6.cloned.1.call-done = bf16[96,6144]{1,0:T(8,128)(2,1)} async-done(((bf16[768,6144]{1,0:T(8,128)(2,1)}), bf16[96,6144]{1,0:T(8,128)(2,1)}) %reduce-scatter.6.cloned.1.call-update) | async-done | bytes 1179664 | tf_op jit(solution)/shard_map/reduce_scatter | solution.py:239
  495.9 4.3 fusion.37
  500.2 58.6 %reduce-scatter.10.cloned.1.call-done = bf16[96,12]{1,0:T(8,128)(2,1)} async-done(((bf16[768,12]{1,0:T(8,128)(2,1)}), bf16[96,12]{1,0:T(8,128)(2,1)}) %reduce-scatter.10.cloned.1.call-update) | async-done | bytes 2320
  559.6 5.7 psum.23
  565.9 40.4 %all-reduce.3.cloned.1.call-done = (bf16[96,6144]{1,0:T(8,128)(2,1)}, bf16[384,768]{1,0:T(8,128)(2,1)}) async-done(((bf16[96,6144]{1,0:T(8,128)(2,1)}, bf16[384,768]{1,0:T(8,128)(2,1)}), (bf16[96,6144]{1,0:T(8,128)(2,1)}, bf16[384,768]{1,0:T(8,128)(2,1)})) %all-reduce.3.cloned.1.call-update) | async-done | bytes 1769488 | tf_op jit(solution)/shard_map/psum | solution.py:261
  606.3 4.6 multiply_subtract_fusion.1
  612.3 4.3 multiply_subtract_fusion
  (126 shorter events, 26.2 us)
Async XLA Ops:
  7.2 3.0 copy-start.3
  7.2 143.7 %all-gather.4.cloned.1.call-start = ((), (), s32[]{:S(2)}) async-start(), calls=%async_computation.3 | async-start | bytes 10616832 | tf_op jit(solution)/shard_map/all_gather | solution.py:221
  10.1 34.5 %copy-start.9 = (bf16[1,197,768]{2,1,0:T(8,128)(2,1)S(1)}, bf16[1,197,768]{2,1,0:T(8,128)(2,1)}, u32[]{:S(2)}) copy-start(bf16[1,197,768]{2,1,0:T(8,128)(2,1)} %param.11) | copy-start | bytes 907780
  10.2 221.0 %all-gather.6.cloned.1.call-start = ((), (), s32[]{:S(2)}) async-start(), calls=%async_computation.4 | async-start | bytes 5308416 | tf_op jit(solution)/shard_map/all_gather | solution.py:222
  11.1 317.8 %reduce-scatter.8.cloned.1.call-start = ((), (), s32[]{:S(2)}) async-start(), calls=%async_computation.6 | async-start | bytes 5308416 | tf_op jit(solution)/shard_map/reduce_scatter | solution.py:253
  155.1 2.2 copy-start.18
  158.0 2.3 copy-start.19
  160.0 76.2 %copy-start.1 = (f32[197,768]{1,0:T(8,128)}, f32[197,768]{1,0:T(8,128)S(1)}, u32[]{:S(2)}) copy-start(f32[197,768]{1,0:T(8,128)S(1)} %get-tuple-element.111) | copy-start | bytes 1815556
  160.3 6.4 %copy-start.13 = (bf16[1,197,768]{2,1,0:T(8,128)(2,1)S(1)}, bf16[1,197,768]{2,1,0:T(8,128)(2,1)}, u32[]{:S(2)}) copy-start(bf16[1,197,768]{2,1,0:T(8,128)(2,1)} %param.12) | copy-start | bytes 907780
  170.4 323.7 %reduce-scatter.6.cloned.1.call-start = ((), (), s32[]{:S(2)}) async-start(), calls=%async_computation.5 | async-start | bytes 10616832 | tf_op jit(solution)/shard_map/reduce_scatter | solution.py:239
  236.2 4.7 copy-start.20
  236.2 4.7 copy-start.14
  259.3 4.9 copy-start.6
  267.1 1.6 copy-start.5
  272.9 285.9 %reduce-scatter.10.cloned.1.call-start = ((), (), s32[]{:S(2)}) async-start(), calls=%async_computation.7 | async-start | bytes 221184
  278.9 327.5 %all-reduce.3.cloned.1.call-start = ((), (), s32[]{:S(2)}) async-start(), calls=%async_computation.8 | async-start | bytes 3538944 | tf_op jit(solution)/shard_map/psum | solution.py:261
  494.2 1.7 copy-start.8
  495.9 69.4 %copy-start.26 = (f32[12,96]{1,0:T(8,128)S(1)}, f32[12,96]{1,0:T(8,128)}, u32[]{:S(2)}) copy-start(f32[12,96]{1,0:T(8,128)} %param.18) | copy-start | bytes 13828
  495.9 69.4 %copy-start.27 = (f32[12,96]{1,0:T(8,128)S(1)}, f32[12,96]{1,0:T(8,128)}, u32[]{:S(2)}) copy-start(f32[12,96]{1,0:T(8,128)} %param.21) | copy-start | bytes 13828
  495.9 110.4 %copy-start.4 = (f32[384,768]{1,0:T(8,128)S(1)}, f32[384,768]{1,0:T(8,128)}, u32[]{:S(2)}) copy-start(f32[384,768]{1,0:T(8,128)} %param.14) | copy-start | bytes 3538948
  606.3 4.6 copy-start
  606.3 4.6 copy-start.16
  606.3 5.7 copy-start.17
  606.3 5.9 copy-start.22
  (14 other events, 17.4 us)
Sparse Core Ops, SparseCore 0:
  10.8 140.0 all-gather.3
  153.6 77.5 all-gather.5
  234.9 94.0 reduce-scatter.7
  332.3 161.7 reduce-scatter.5
  497.8 60.9 reduce-scatter.9
  561.2 45.0 all-reduce.2
where the time goes:
time: 624 us; the launch traced here: 623 us
  waiting for transfers between devices  481 us (77%)
  matrix products  54.9 us (9%)
  blocking collectives  38.9 us (6%)
  other arithmetic  20.4 us (3%)
  between operations  14.6 us (2%)
  local copies, waits for them, and re-layouts  13.3 us (2%)
    reduce_scatter x1, waiting for transfers between devices, local(): lax.psum_scatter(jnp.concatenate([column_part(act_one, grad_proj), column...  165 us
    all_gather x1, waiting for transfers between devices, local(): lax.all_gather(halves[0], 'shard', axis=0, tiled=True)  106 us
    all_gather x1, waiting for transfers between devices, local(): lax.all_gather(halves[1], 'shard', axis=0, tiled=True)  60.5 us
    unnamed x7, waiting for transfers between devices  58.7 us
    reduce_scatter x1, waiting for transfers between devices, local(): lax.psum_scatter(grad_down_local.astype(jnp.bfloat16), 'shard', scatter_d...  50 us
    psum x1, waiting for transfers between devices, local(): lax.psum(owned_in, 'rep').astype(jnp.float32)  40.4 us
    all_gather x1, blocking collectives, local(): lax.all_gather(halves[2], 'shard', axis=1, tiled=True)  33.3 us
    dot_general x4, matrix products, times_transposed(): lax.dot_general(left, right, (((1,), (1,)), ((), ())), preferred_element_...  15.7 us
  transfers between devices with their start and end apart: 6, of which 6 were waited for; matrix products, arithmetic and copies ran while one was open for 12% of the time, Pallas kernels for 0%

commit v1 on v0

--- a/solution.py
+++ b/solution.py
@@ -217,9 +217,32 @@
     square_vectors,
 ):
     halves = (to_half(weights_in), to_half(weights_down), to_half(vectors))
+
+    def space_extend(xx):
+        z_new = jax.lax.axis_size("shard")
+        y2 = jax.lax.axis_index("shard")
+        earlier, side_arr, now = (z_new, y2, xx.shape[0])
+        vals = [(to_i, (to_i + 1) % earlier) for to_i in range(earlier)]
+        shelf = [(to_i, (to_i - 1) % earlier) for to_i in range(earlier)]
+        arr_out = jnp.zeros((*xx.shape[:0], earlier * now, *xx.shape[1:]), xx.dtype)
+        arr_out = lax.dynamic_update_slice_in_dim(arr_out, xx, side_arr * now, axis=0)
+        out_arr = r1 = xx
+        vec_out = earlier // 2
+        for dd in [*range(1, vec_out + 1)]:
+            out_arr = jax.lax.ppermute(out_arr, "shard", vals)
+            arr_out = lax.dynamic_update_slice_in_dim(
+                arr_out, out_arr, (side_arr - dd) % earlier * now, axis=0
+            )
+            if dd < earlier - vec_out:
+                r1 = jax.lax.ppermute(r1, "shard", shelf)
+                arr_out = lax.dynamic_update_slice_in_dim(
+                    arr_out, r1, (side_arr + dd) % earlier * now, axis=0
+                )
+        return arr_out
+
     forward_set = (
         lax.all_gather(halves[0], "shard", axis=0, tiled=True),
-        lax.all_gather(halves[1], "shard", axis=0, tiled=True),
+        space_extend(halves[1]),
         lax.all_gather(halves[2], "shard", axis=1, tiled=True),
     )
     block_out, saved = forward_pass(images, forward_set[0], forward_set[1], forward_set[2])

time: 624 us -> 682 us (1.093)
  waiting for transfers between devices: 481 us -> 510 us
  starting transfers between devices: 0.65 us -> 18.8 us
  local copies, waits for them, and re-layouts: 13.3 us -> 22.8 us
    ppermute x0 -> x7, waiting for transfers between devices: none -> 95.6 us  [the longest x4 95.6 us: space_extend(): out_arr = jax.lax.ppermute(out_arr, 'shard', vals)]
    reduce_scatter x1, waiting for transfers between devices: 50 us -> 0.02 us  [local(): lax.psum_scatter(grad_down_local.astype(jnp.bfloat16), 'shard', scatter_d...]
    ppermute x0 -> x7, starting transfers between devices: none -> 18.3 us  [the longest x3 10.1 us: space_extend(): r1 = jax.lax.ppermute(r1, 'shard', shelf)]
    reduce_scatter x1, waiting for transfers between devices: 165 us -> 152 us  [local(): lax.psum_scatter(jnp.concatenate([column_part(act_one, grad_proj), column...]
    dynamic_update_slice x0 -> x7, local copies, waits for them, and re-layouts: none -> 7.2 us  [the longest x4 4.54 us: space_extend(): lax.dynamic_update_slice_in_dim(arr_out, out_arr, (side_arr - dd) % earli...]
  transfers between devices with their start and end apart: 6 -> 13, of which waited for: 6 -> 9; matrix products, arithmetic and copies ran while one was open for 12% -> 12% of each run, Pallas kernels for 0% -> 0%
where the time goes in v1:
time: 682 us; the launch traced here: 681 us
  waiting for transfers between devices  510 us (75%)
  matrix products  55 us (8%)
  blocking collectives  39.1 us (6%)
  local copies, waits for them, and re-layouts  22.8 us (3%)
  other arithmetic  21 us (3%)
  starting transfers between devices  18.8 us (3%)
  between operations  14.6 us (2%)
    reduce_scatter x1, waiting for transfers between devices, local(): lax.psum_scatter(jnp.concatenate([column_part(act_one, grad_proj), column...  152 us
    all_gather x1, waiting for transfers between devices, local(): lax.all_gather(halves[0], 'shard', axis=0, tiled=True)  102 us
    ppermute x4, waiting for transfers between devices, space_extend(): out_arr = jax.lax.ppermute(out_arr, 'shard', vals)  95.6 us
    all_gather x1, waiting for transfers between devices, local(): lax.all_gather(halves[1], 'shard', axis=0, tiled=True)  60.5 us
    unnamed x7, waiting for transfers between devices  58.7 us
    psum x1, waiting for transfers between devices, local(): lax.psum(owned_in, 'rep').astype(jnp.float32)  40.4 us
    all_gather x1, blocking collectives, local(): lax.all_gather(halves[2], 'shard', axis=1, tiled=True)  33.5 us
    dot_general x4, matrix products, times_transposed(): lax.dot_general(left, right, (((1,), (1,)), ((), ())), preferred_element_...  15.7 us
  transfers between devices with their start and end apart: 13, of which 9 were waited for; matrix products, arithmetic and copies ran while one was open for 12% of the time, Pallas kernels for 0%

profile of v1, /device:TPU:0, one launch (start us, length us, event | category | flops | bytes accessed | tf_op | source)
XLA Modules:
  0.0 681.3 jit_solution(11197868036022037570)
XLA Ops:
  14.6 33.5 %all-gather = bf16[8,96,12]{1,2,0:T(8,128)(2,1)S(1)} all-gather(bf16[1,96,12]{1,2,0:T(8,128)(2,1)S(1)} %convert_bitcast_fusion.1), channel_id=1, replica_groups=mesh['shard'=8,'rep'=4] {'shard'}, dimensions={0}, use_global_device_ids=true | all-gather | bytes 20736 | tf_op jit(solution)/shard_map/all_gather | solution.py:246
  48.6 102.4 %all-gather.4.cloned.1.call-done = bf16[768,6144]{1,0:T(8,128)(2,1)} async-done(((bf16[96,6144]{1,0:T(8,128)(2,1)}), bf16[768,6144]{1,0:T(8,128)(2,1)}) %all-gather.4.cloned.1.call-update) | async-done | bytes 9437200 | tf_op jit(solution)/shard_map/all_gather | solution.py:244
  151.0 3.0 fusion.10
  160.5 5.4 multiply_convert_fusion.1
  166.9 3.6 convolution_convert_fusion
  170.8 60.5 %all-gather.6.cloned.1.call-done = bf16[3072,768]{1,0:T(8,128)(2,1)} async-done(((bf16[384,768]{1,0:T(8,128)(2,1)}), bf16[3072,768]{1,0:T(8,128)(2,1)}) %all-gather.6.cloned.1.call-update) | async-done | bytes 4718608 | tf_op jit(solution)/shard_map/all_gather | solution.py:251
  231.3 5.0 fusion.90
  236.3 4.7 multiply_reduce_fusion.2
  254.7 4.7 fusion.30
  259.3 4.8 fusion.86
  268.8 4.2 pad_maximum_fusion
  274.8 4.0 collective-permute-start.1
  278.7 26.1 %collective-permute-done = bf16[384,768]{1,0:T(8,128)(2,1)S(1)} collective-permute-done((bf16[384,768]{1,0:T(8,128)(2,1)S(1)}, bf16[384,768]{1,0:T(8,128)(2,1)S(1)}, u32[]{:S(2)}, u32[]{:S(2)}) %collective-permute-start) | collective-permute-done | bytes 589856 | tf_op jit(solution)/shard_map/ppermute | solution.py:232
  309.8 26.8 %collective-permute-done.2 = bf16[384,768]{1,0:T(8,128)(2,1)S(1)} collective-permute-done((bf16[384,768]{1,0:T(8,128)(2,1)S(1)}, bf16[384,768]{1,0:T(8,128)(2,1)S(1)}, u32[]{:S(2)}, u32[]{:S(2)}) %collective-permute-start.2) | collective-permute-done | bytes 589856 | tf_op jit(solution)/shard_map/ppermute | solution.py:232
  339.2 3.7 collective-permute-start.5
  344.9 23.9 %collective-permute-done.4 = bf16[384,768]{1,0:T(8,128)(2,1)S(1)} collective-permute-done((bf16[384,768]{1,0:T(8,128)(2,1)S(1)}, bf16[384,768]{1,0:T(8,128)(2,1)S(1)}, u32[]{:S(2)}, u32[]{:S(2)}) %collective-permute-start.4) | collective-permute-done | bytes 589856 | tf_op jit(solution)/shard_map/ppermute | solution.py:232
  375.7 18.8 %collective-permute-done.6 = bf16[384,768]{1,0:T(8,128)(2,1)S(1)} collective-permute-done((bf16[384,768]{1,0:T(8,128)(2,1)S(1)}, bf16[384,768]{1,0:T(8,128)(2,1)S(1)}, u32[]{:S(2)}, u32[]{:S(2)}) %collective-permute-start.6) | collective-permute-done | bytes 589856 | tf_op jit(solution)/shard_map/ppermute | solution.py:232
  395.3 3.5 fusion.56
  400.1 152.4 %reduce-scatter.6.cloned.1.call-done = bf16[96,6144]{1,0:T(8,128)(2,1)} async-done(((bf16[768,6144]{1,0:T(8,128)(2,1)}), bf16[96,6144]{1,0:T(8,128)(2,1)}) %reduce-scatter.6.cloned.1.call-update) | async-done | bytes 1179664 | tf_op jit(solution)/shard_map/reduce_scatter | solution.py:262
  554.3 4.4 fusion.37
  558.7 58.6 %reduce-scatter.10.cloned.1.call-done = bf16[96,12]{1,0:T(8,128)(2,1)} async-done(((bf16[768,12]{1,0:T(8,128)(2,1)}), bf16[96,12]{1,0:T(8,128)(2,1)}) %reduce-scatter.10.cloned.1.call-update) | async-done | bytes 2320
  618.1 5.7 psum.23
  624.4 40.4 %all-reduce.3.cloned.1.call-done = (bf16[96,6144]{1,0:T(8,128)(2,1)}, bf16[384,768]{1,0:T(8,128)(2,1)}) async-done(((bf16[96,6144]{1,0:T(8,128)(2,1)}, bf16[384,768]{1,0:T(8,128)(2,1)}), (bf16[96,6144]{1,0:T(8,128)(2,1)}, bf16[384,768]{1,0:T(8,128)(2,1)})) %all-reduce.3.cloned.1.call-update) | async-done | bytes 1769488 | tf_op jit(solution)/shard_map/psum | solution.py:284
  664.8 7.2 %multiply_subtract_fusion = (f32[96,6144]{1,0:T(8,128)}, f32[96,6144]{1,0:T(8,128)}, f32[96,6144]{1,0:T(8,128)}, f32[96,6144]{1,0:T(8,128)}) fusion(f32[96,6144]{1,0:T(8,128)S(1)} %copy-done, f32[96,6144]{1,0:T(8,128)} %param.16, f32[96,6144]{1,0:T(8,128)} %param.19, bf16[96,6144]{1,0:T(8,128)(2,1)} %get-tuple-element.86), kind=kLoop, calls=%fused_computation.29 | loop fusion | flops 9437184 | bytes 17694720 | tf_op jit(solution)/shard_map/sub | solution.py:202
  (156 shorter events, 59.6 us)
Async XLA Ops:
  7.2 143.8 %all-gather.4.cloned.1.call-start = ((), (), s32[]{:S(2)}) async-start(), calls=%async_computation.3 | async-start | bytes 10616832 | tf_op jit(solution)/shard_map/all_gather | solution.py:244
  10.1 221.2 %all-gather.6.cloned.1.call-start = ((), (), s32[]{:S(2)}) async-start(), calls=%async_computation.4 | async-start | bytes 5308416 | tf_op jit(solution)/shard_map/all_gather | solution.py:251
  11.3 36.9 %copy-start.11 = (bf16[1,197,768]{2,1,0:T(8,128)(2,1)S(1)}, bf16[1,197,768]{2,1,0:T(8,128)(2,1)}, u32[]{:S(2)}) copy-start(bf16[1,197,768]{2,1,0:T(8,128)(2,1)} %param.11) | copy-start | bytes 907780
  14.5 385.6 %reduce-scatter.8.cloned.1.call-start = ((), (), s32[]{:S(2)}) async-start(), calls=%async_computation.6 | async-start | bytes 5308416 | tf_op jit(solution)/shard_map/reduce_scatter | solution.py:276
  160.3 76.0 %copy-start.1 = (f32[197,768]{1,0:T(8,128)}, f32[197,768]{1,0:T(8,128)S(1)}, u32[]{:S(2)}) copy-start(f32[197,768]{1,0:T(8,128)S(1)} %get-tuple-element.113) | copy-start | bytes 1815556
  170.6 381.9 %reduce-scatter.6.cloned.1.call-start = ((), (), s32[]{:S(2)}) async-start(), calls=%async_computation.5 | async-start | bytes 10616832 | tf_op jit(solution)/shard_map/reduce_scatter | solution.py:262
  272.9 66.2 %copy-start.17 = (bf16[1,197,768]{2,1,0:T(8,128)(2,1)S(1)}, bf16[1,197,768]{2,1,0:T(8,128)(2,1)}, u32[]{:S(2)}) copy-start(bf16[1,197,768]{2,1,0:T(8,128)(2,1)} %param.12) | copy-start | bytes 907780
  273.0 344.3 %reduce-scatter.10.cloned.1.call-start = ((), (), s32[]{:S(2)}) async-start(), calls=%async_computation.7 | async-start | bytes 221184
  274.0 30.9 %collective-permute-start = (bf16[384,768]{1,0:T(8,128)(2,1)S(1)}, bf16[384,768]{1,0:T(8,128)(2,1)S(1)}, u32[]{:S(2)}, u32[]{:S(2)}) collective-permute-start(bf16[384,768]{1,0:T(8,128)(2,1)S(1)} %copy-done.18), channel_id=1, source_target_pairs={{0,4},{4,8},{8,12},{12,16},{16,20},{20,24},{24,28},{28,0},{1,5},{5... | collective-permute-start | bytes 1769480 | tf_op jit(solution)/shard_map/ppermute | solution.py:232
  274.8 32.6 %collective-permute-start.1 = (bf16[384,768]{1,0:T(8,128)(2,1)S(1)}, bf16[384,768]{1,0:T(8,128)(2,1)S(1)}, u32[]{:S(2)}, u32[]{:S(2)}) collective-permute-start(bf16[384,768]{1,0:T(8,128)(2,1)S(1)} %copy-done.18), channel_id=1, source_target_pairs={{0,28},{4,0},{8,4},{12,8},{16,12},{20,16},{24,20},{28,24},{1,29},{... | collective-permute-start | bytes 1769480 | tf_op jit(solution)/shard_map/ppermute | solution.py:237
  304.9 31.7 %copy-start.26 = (bf16[384,768]{1,0:T(8,128)(2,1)}, bf16[384,768]{1,0:T(8,128)(2,1)S(1)}, u32[]{:S(2)}) copy-start(bf16[384,768]{1,0:T(8,128)(2,1)S(1)} %collective-permute-done) | copy-start | bytes 1769476
  304.9 31.7 %collective-permute-start.2 = (bf16[384,768]{1,0:T(8,128)(2,1)S(1)}, bf16[384,768]{1,0:T(8,128)(2,1)S(1)}, u32[]{:S(2)}, u32[]{:S(2)}) collective-permute-start(bf16[384,768]{1,0:T(8,128)(2,1)S(1)} %collective-permute-done), channel_id=1, source_target_pairs={{0,4},{4,8},{8,12},{12,16},{16,20},{20,24},{24,28},{28,0},{1,5},{5... | collective-permute-start | bytes 1769480 | tf_op jit(solution)/shard_map/ppermute | solution.py:232
  307.4 31.9 %collective-permute-start.3 = (bf16[384,768]{1,0:T(8,128)(2,1)S(1)}, bf16[384,768]{1,0:T(8,128)(2,1)S(1)}, u32[]{:S(2)}, u32[]{:S(2)}) collective-permute-start(bf16[384,768]{1,0:T(8,128)(2,1)S(1)} %collective-permute-done.1), channel_id=1, source_target_pairs={{0,28},{4,0},{8,4},{12,8},{16,12},{20,16},{24,20},{28,24},{1,29},{... | collective-permute-start | bytes 1769480 | tf_op jit(solution)/shard_map/ppermute | solution.py:237
  336.6 32.2 %collective-permute-start.4 = (bf16[384,768]{1,0:T(8,128)(2,1)S(1)}, bf16[384,768]{1,0:T(8,128)(2,1)S(1)}, u32[]{:S(2)}, u32[]{:S(2)}) collective-permute-start(bf16[384,768]{1,0:T(8,128)(2,1)S(1)} %collective-permute-done.2), channel_id=1, source_target_pairs={{0,4},{4,8},{8,12},{12,16},{16,20},{20,24},{24,28},{28,0},{1,5},{5... | collective-permute-start | bytes 1769480 | tf_op jit(solution)/shard_map/ppermute | solution.py:232
  339.2 35.5 %collective-permute-start.5 = (bf16[384,768]{1,0:T(8,128)(2,1)S(1)}, bf16[384,768]{1,0:T(8,128)(2,1)S(1)}, u32[]{:S(2)}, u32[]{:S(2)}) collective-permute-start(bf16[384,768]{1,0:T(8,128)(2,1)S(1)} %collective-permute-done.3), channel_id=1, source_target_pairs={{0,28},{4,0},{8,4},{12,8},{16,12},{20,16},{24,20},{28,24},{1,29},{... | collective-permute-start | bytes 1769480 | tf_op jit(solution)/shard_map/ppermute | solution.py:237
  368.8 25.7 %collective-permute-start.6 = (bf16[384,768]{1,0:T(8,128)(2,1)S(1)}, bf16[384,768]{1,0:T(8,128)(2,1)S(1)}, u32[]{:S(2)}, u32[]{:S(2)}) collective-permute-start(bf16[384,768]{1,0:T(8,128)(2,1)S(1)} %collective-permute-done.4), channel_id=1, source_target_pairs={{0,4},{4,8},{8,12},{12,16},{16,20},{20,24},{24,28},{28,0},{1,5},{5... | collective-permute-start | bytes 1769480 | tf_op jit(solution)/shard_map/ppermute | solution.py:232
  373.0 22.3 %copy-start.14 = (bf16[1,197,768]{2,1,0:T(8,128)(2,1)S(1)}, bf16[1,197,768]{2,1,0:T(8,128)(2,1)}, u32[]{:S(2)}) copy-start(bf16[1,197,768]{2,1,0:T(8,128)(2,1)} %param.11) | copy-start | bytes 907780
  373.0 22.3 %copy-start.28 = (bf16[1,197,12,64]{1,3,2,0:T(8,128)(2,1)S(1)}, bf16[1,197,12,64]{1,3,2,0:T(8,128)(2,1)}, u32[]{:S(2)}) copy-start(bf16[1,197,12,64]{1,3,2,0:T(8,128)(2,1)} %copy-done.27) | copy-start | bytes 907780
  373.0 22.3 %copy-start.33 = (bf16[12,64,197]{2,1,0:T(8,128)(2,1)S(1)}, bf16[12,64,197]{2,1,0:T(8,128)(2,1)}, u32[]{:S(2)}) copy-start(bf16[12,64,197]{2,1,0:T(8,128)(2,1)} %fusion.30) | copy-start | bytes 907780
  373.0 22.3 %copy-start.35 = (bf16[1,197,12,64]{1,3,2,0:T(8,128)(2,1)S(1)}, bf16[1,197,12,64]{1,3,2,0:T(8,128)(2,1)}, u32[]{:S(2)}) copy-start(bf16[1,197,12,64]{1,3,2,0:T(8,128)(2,1)} %get-tuple-element.109) | copy-start | bytes 907780
  400.0 264.7 %all-reduce.3.cloned.1.call-start = ((), (), s32[]{:S(2)}) async-start(), calls=%async_computation.8 | async-start | bytes 3538944 | tf_op jit(solution)/shard_map/psum | solution.py:284
  554.3 69.5 %copy-start.30 = (f32[12,96]{1,0:T(8,128)S(1)}, f32[12,96]{1,0:T(8,128)}, u32[]{:S(2)}) copy-start(f32[12,96]{1,0:T(8,128)} %param.18) | copy-start | bytes 13828
  554.3 69.5 %copy-start.31 = (f32[12,96]{1,0:T(8,128)S(1)}, f32[12,96]{1,0:T(8,128)}, u32[]{:S(2)}) copy-start(f32[12,96]{1,0:T(8,128)} %param.21) | copy-start | bytes 13828
  554.3 110.5 %copy-start = (f32[96,6144]{1,0:T(8,128)S(1)}, f32[96,6144]{1,0:T(8,128)}, u32[]{:S(2)}) copy-start(f32[96,6144]{1,0:T(8,128)} %param.13) | copy-start | bytes 7077892
  (25 other events, 77.0 us)
Sparse Core Ops, SparseCore 0:
  10.7 140.2 all-gather.3
  153.8 77.4 all-gather.5
  234.9 142.9 reduce-scatter.7
  381.4 171.0 reduce-scatter.5
  556.2 61.0 reduce-scatter.9
  619.6 45.0 all-reduce.2
